TPU v7x, 32 devices: a whole 2x2x4 slice. The times are simulated.
32 devices in a mesh: dp: 4 (over z), fsdp: 8 (over y, x, core).
Axes of the slice: x: 2, y: 2, z: 4, core: 2. Of those that a mesh axis runs over, the one named last changes fastest.
Arguments:
- frames: bfloat16 [64, 256, 1536], P(('dp', 'fsdp')), may hold values from -6 to 6
- lengths: int32 [64], P(('dp', 'fsdp')), may hold values from 1 to 256, as said below
- norm_in_gain: float32 [1536], replicated, may hold values from 0.1 to 1.9
- w_in: bfloat16 [1536, 3072], P('fsdp'), may hold values from -0.15625 to 0.15625
- dw_kernel: float32 [31, 1536], replicated, may hold values from -1 to 1
- norm_mid_gain: float32 [1536], replicated, may hold values from 0.1 to 1.9
- w_out: bfloat16 [1536, 1536], P('fsdp'), may hold values from -0.15625 to 0.15625
Outputs:
- module_out: bfloat16 [64, 256, 1536], P(('dp', 'fsdp'))
Inputs may be any that keep to these rules, and one draw needn't show every extreme that they name: Utterance u has ceil(lengths[u] / 64) live blocks. Two devices of the same dp index whose fsdp indices differ by half of 8 hold at most 10 live blocks together; in every dp group some such pair holds exactly 10, one device of it having all 8 blocks live with every utterance of length 256.
All inputs are finite; a program needn't handle non-finite values.
Results may differ from a plain program's by a relative error of at most 0.0066.
Values may be sent and summed in bfloat16 or wider, within the bound.
A program may use at most 128 MiB of HBM per device.

v0:
```python
import jax
import jax.numpy as jnp
from jax import lax
from jax.sharding import PartitionSpec as P


def layer_norm(values, gain_vec):
    center = values - jnp.mean(values, axis=-1, keepdims=True)
    spread = jnp.mean(center * center, axis=-1, keepdims=True)
    return center * lax.rsqrt(spread + 1e-05) * gain_vec


def expand_in(flat_rows, w_in):
    model_width = flat_rows.shape[1]
    projected = jnp.dot(
        flat_rows,
        lax.all_gather(w_in, "fsdp", axis=0, tiled=True),
        preferred_element_type=jnp.float32,
    )
    return (projected[:, :model_width] * jax.nn.sigmoid(projected[:, model_width:])).astype(
        jnp.bfloat16
    )


def contract_out(flat_rows, w_out):
    projected = jnp.dot(
        flat_rows,
        lax.all_gather(w_out, "fsdp", axis=0, tiled=True),
        preferred_element_type=jnp.float32,
    )
    return projected.astype(jnp.bfloat16)


def on_device(frames, lengths, norm_in_gain, w_in, dw_kernel, norm_mid_gain, w_out):
    utt_count, frame_span, model_width = frames.shape
    positions = jnp.arange(frame_span, dtype=jnp.int32)
    valid = (positions[None, :] < lengths[:, None])[:, :, None]
    normed = layer_norm(frames.astype(jnp.float32), norm_in_gain).astype(jnp.bfloat16)

    def apply_rows(values, compute):
        return compute(values.reshape(utt_count * frame_span, model_width)).reshape(
            utt_count, frame_span, -1
        )

    def first_section(flat_rows):
        return expand_in(flat_rows, w_in)

    def last_section(flat_rows):
        return contract_out(flat_rows, w_out)

    gated = apply_rows(normed, first_section)
    gated = jnp.where(valid, gated, jnp.zeros((), jnp.bfloat16))
    taps = dw_kernel.shape[0]
    half_k = (taps - 1) // 2
    padded = jnp.pad(gated, ((0, 0), (half_k, half_k), (0, 0)))
    convolved = jnp.zeros((utt_count, frame_span, model_width), jnp.float32)
    for offset in range(taps):
        convolved = convolved + padded[:, offset : offset + frame_span, :] * dw_kernel[offset]
    middle = layer_norm(convolved, norm_mid_gain)
    middle = (middle * jax.nn.sigmoid(middle)).astype(jnp.bfloat16)
    result = apply_rows(middle, last_section)
    return jnp.where(valid, result, jnp.zeros((), jnp.bfloat16))


def solution(mesh):
    return jax.shard_map(
        on_device,
        mesh=mesh,
        in_specs=(
            P(("dp", "fsdp"), None, None),
            P(("dp", "fsdp")),
            P(),
            P("fsdp", None),
            P(),
            P(),
            P("fsdp", None),
        ),
        out_specs=P(("dp", "fsdp"), None, None),
        check_vma=False,
    )
```

profile of v0, /device:TPU:0, one launch (start us, length us, event | category | flops | bytes accessed | tf_op | source)
XLA Modules:
  0.0 124.5 jit_solution(6595838935682310830)
XLA Ops:
  6.5 0.0 copy-start
  6.5 0.0 copy-start.3
  6.5 0.0 copy-start.1
  6.5 0.0 all-gather.3.cloned.1.call-start
  6.5 0.7 all-gather.3.cloned.1.call-update
  7.3 0.0 all-gather.5.cloned.1.call-start
  7.3 0.7 all-gather.5.cloned.1.call-update
  8.0 1.5 %slice_reduce_fusion.29 = (f32[1536]{0:T(1024)S(1)}, f32[1536]{0:T(1024)S(1)}, f32[1536]{0:T(1024)S(1)}, f32[1536]{0:T(1024)S(1)}, f32[1536]{0:T(1024)S(1)}, /*i...) fusion(f32[31,1536]{1,0:T(8,128)} %param.11), kind=kLoop, calls=%fused_computation.56 | loop fusion | bytes 147456 | tf_op jit(solution)/shard_map/slice | solution.py:58
  9.5 2.1 %slice_reduce_fusion.30 = (f32[1536]{0:T(1024)S(1)}, f32[1536]{0:T(1024)S(1)}, f32[1536]{0:T(1024)S(1)}, f32[1536]{0:T(1024)S(1)}, f32[1536]{0:T(1024)S(1)}, /*i...) fusion(f32[31,1536]{1,0:T(8,128)} %param.11), kind=kLoop, calls=%fused_computation.57 | loop fusion | bytes 233472 | tf_op jit(solution)/shard_map/slice | solution.py:58
  11.6 0.0 copy-done
  11.6 0.3 convert_reduce_fusion
  11.9 0.0 copy-done.3
  11.9 0.1 iota_compare_fusion
  12.0 0.6 fusion.2
  12.5 0.0 copy-done.1
  12.5 0.5 fusion.4
  13.1 57.6 %all-gather.3.cloned.1.call-done = bf16[1536,3072]{1,0:T(8,128)(2,1)} async-done(((bf16[192,3072]{1,0:T(8,128)(2,1)}), bf16[1536,3072]{1,0:T(8,128)(2,1)}) %all-gather.3.cloned.1.call-update) | async-done | bytes 9437200 | tf_op jit(solution)/shard_map/all_gather | solution.py:17
  70.7 7.6 %fusion.11 = f32[512,3072]{1,0:T(8,128)S(1)} fusion(bf16[512,1536]{1,0:T(8,128)(2,1)S(1)} %bitcast.9, bf16[1536,3072]{1,0:T(8,128)(2,1)} %all-gather.3.cloned.1.call-done), kind=kOutput, calls=%fused_computation.64 | convolution fusion | flops 4831838208 | bytes 17301504 | tf_op jit(solution)/shard_map/dot_general | solution.py:15
  78.3 0.8 fusion.9
  79.1 0.2 broadcast_select_fusion.1
  79.3 0.0 copy-start.2
  79.3 13.8 %fusion.10 = (f32[2,256]{1,0:T(2,128)S(1)}, f32[2,256,1536]{2,1,0:T(8,128)S(1)}) fusion(f32[1536]{0:T(1024)S(1)} %get-tuple-element.34, f32[1536]{0:T(1024)S(1)} %get-tuple-element.35, f32[1536]{0:T(1024)S(1)} %get-tuple-element.6, f32[1536]{0:T(1024)S(1)} %get-tuple-element.7, f32[1536]{0:T(1024)S(1)} %get-tuple-element.8, f32[1536]{0:T(1024)S(1)} %get-tuple-element.9, ...), kind=kLoop, calls=%fused_computation.63 | loop fusion | flops 73137664 | bytes 4911104 | tf_op jit(solution)/shard_map/reduce_sum | solution.py:8
  93.1 0.5 multiply_reduce_fusion
  93.5 0.0 copy-done.2
  93.6 1.1 multiply_convert_fusion
  94.6 16.7 %all-gather.5.cloned.1.call-done = bf16[1536,1536]{1,0:T(8,128)(2,1)} async-done(((bf16[192,1536]{1,0:T(8,128)(2,1)}), bf16[1536,1536]{1,0:T(8,128)(2,1)}) %all-gather.5.cloned.1.call-update) | async-done | bytes 4718608 | tf_op jit(solution)/shard_map/all_gather | solution.py:28
  111.4 5.0 %convolution_convert_fusion = bf16[512,1536]{1,0:T(8,128)(2,1)S(1)} fusion(bf16[512,1536]{1,0:T(8,128)(2,1)S(1)} %bitcast.11, bf16[1536,1536]{1,0:T(8,128)(2,1)} %all-gather.5.cloned.1.call-done), kind=kOutput, calls=%fused_computation.16 | convolution fusion | flops 2416705536 | bytes 7864320 | tf_op jit(solution)/shard_map/dot_general | solution.py:26
  116.3 1.3 %broadcast_select_fusion = bf16[2,256,1536]{2,1,0:T(8,128)(2,1)} fusion(bf16[2,256,1536]{2,1,0:T(8,128)(2,1)S(1)} %bitcast.10, pred[2,256]{1,0:T(4,128)(4,1)S(1)} %iota_compare_fusion), kind=kLoop, calls=%fused_computation.25 | loop fusion | flops 786432 | bytes 3146240 | tf_op jit(solution)/shard_map/jit(_where)/select_n | solution.py:62
  (4 shorter events, 0.0 us)
Async XLA Ops:
  6.5 5.1 %copy-start = (bf16[2,256,1536]{2,1,0:T(8,128)(2,1)S(1)}, bf16[2,256,1536]{2,1,0:T(8,128)(2,1)}, u32[]{:S(2)}) copy-start(bf16[2,256,1536]{2,1,0:T(8,128)(2,1)} %param.7) | copy-start | bytes 4718596
  6.5 5.3 %copy-start.3 = (s32[2]{0:T(128)S(1)}, s32[2]{0:T(128)}, u32[]{:S(2)}) copy-start(s32[2]{0:T(128)} %param.8) | copy-start | bytes 28
  6.5 6.0 %copy-start.1 = (f32[1536]{0:T(1024)S(1)}, f32[1536]{0:T(1024)}, u32[]{:S(2)}) copy-start(f32[1536]{0:T(1024)} %param.9) | copy-start | bytes 18436
  6.5 64.1 %all-gather.3.cloned.1.call-start = ((), (), s32[]{:S(2)}) async-start(), calls=%async_computation | async-start | bytes 10616832 | tf_op jit(solution)/shard_map/all_gather | solution.py:17
  7.3 104.1 %all-gather.5.cloned.1.call-start = ((), (), s32[]{:S(2)}) async-start(), calls=%async_computation.1 | async-start | bytes 5308416 | tf_op jit(solution)/shard_map/all_gather | solution.py:28
  79.3 14.3 %copy-start.2 = (f32[1536]{0:T(1024)S(1)}, f32[1536]{0:T(1024)}, u32[]{:S(2)}) copy-start(f32[1536]{0:T(1024)} %param.12) | copy-start | bytes 18436
Sparse Core Ops, SparseCore 0:
  9.2 61.4 all-gather.2
  72.6 38.7 all-gather.4
where the time goes:
time: 125 us; the launch traced here: 124 us
  waiting for transfers between devices  75.7 us (61%)
  other arithmetic  19.1 us (15%)
  between operations  13.5 us (11%)
  matrix products  12.5 us (10%)
  local copies, waits for them, and re-layouts  3.59 us (3%)
    all_gather x1, waiting for transfers between devices, expand_in(): lax.all_gather(w_in, 'fsdp', axis=0, tiled=True)  57.6 us
    all_gather x1, waiting for transfers between devices, contract_out(): lax.all_gather(w_out, 'fsdp', axis=0, tiled=True)  16.7 us
    reduce_sum x2, other arithmetic, layer_norm(): center = values - jnp.mean(values, axis=-1, keepdims=True)  14.1 us
    dot_general x1, matrix products, expand_in(): jnp.dot(flat_rows, lax.all_gather(w_in, 'fsdp', axis=0, tiled=True), pref...  7.59 us
    dot_general x1, matrix products, contract_out(): jnp.dot(flat_rows, lax.all_gather(w_out, 'fsdp', axis=0, tiled=True), pre...  4.95 us
    slice x2, local copies, waits for them, and re-layouts, on_device(): dw_kernel[offset]  3.57 us
  transfers between devices with their start and end apart: 2, of which 2 were waited for; matrix products, arithmetic and copies ran while one was open for 23% of the time, Pallas kernels for 0%

commit v1 on v0

--- a/solution.py
+++ b/solution.py
@@ -2,6 +2,25 @@
 import jax.numpy as jnp
 from jax import lax
 from jax.sharding import PartitionSpec as P
+
+
+def collect(array, axis, dim):
+    size, here, rows = (lax.axis_size(axis), lax.axis_index(axis), array.shape[dim])
+    right = [(i, (i + 1) % size) for i in range(size)]
+    downward = [(i, (i - 1) % size) for i in range(size)]
+    out = jnp.zeros((*array.shape[:dim], size * rows, *array.shape[dim + 1 :]), array.dtype)
+    out = lax.dynamic_update_slice_in_dim(out, array, here * rows, axis=dim)
+    from_left = from_right = array
+    half = size // 2
+    for lap in range(1, half + 1):
+        from_left = lax.ppermute(from_left, axis, right)
+        out = lax.dynamic_update_slice_in_dim(out, from_left, (here - lap) % size * rows, axis=dim)
+        if lap < size - half:
+            from_right = lax.ppermute(from_right, axis, downward)
+            out = lax.dynamic_update_slice_in_dim(
+                out, from_right, (here + lap) % size * rows, axis=dim
+            )
+    return out
 
 
 def layer_norm(values, gain_vec):
@@ -12,11 +31,7 @@
 
 def expand_in(flat_rows, w_in):
     model_width = flat_rows.shape[1]
-    projected = jnp.dot(
-        flat_rows,
-        lax.all_gather(w_in, "fsdp", axis=0, tiled=True),
-        preferred_element_type=jnp.float32,
-    )
+    projected = jnp.dot(flat_rows, collect(w_in, "fsdp", 0), preferred_element_type=jnp.float32)
     return (projected[:, :model_width] * jax.nn.sigmoid(projected[:, model_width:])).astype(
         jnp.bfloat16
     )

time: 125 us -> 159 us (1.27)
  waiting for transfers between devices: 75.7 us -> 97.7 us
  starting transfers between devices: 0.04 us -> 9.81 us
  matrix products: 12.5 us -> 9.97 us
  local copies, waits for them, and re-layouts: 3.59 us -> 5.35 us
    ppermute x0 -> x7, waiting for transfers between devices: none -> 97.6 us  [the longest x4 94.1 us: collect(): from_left = lax.ppermute(from_left, axis, right)]
    all_gather x1 -> x0, waiting for transfers between devices: 57.6 us -> none  [expand_in(): lax.all_gather(w_in, 'fsdp', axis=0, tiled=True)]
    all_gather x1, waiting for transfers between devices: 16.7 us -> 0.02 us  [contract_out(): lax.all_gather(w_out, 'fsdp', axis=0, tiled=True)]
    ppermute x0 -> x7, starting transfers between devices: none -> 9.81 us  [the longest x3 8.38 us: collect(): from_right = lax.ppermute(from_right, axis, downward)]
    dynamic_update_slice x0 -> x8, local copies, waits for them, and re-layouts: none -> 3.57 us  [the longest x4 3.06 us: collect(): lax.dynamic_update_slice_in_dim(out, from_left, (here - lap) % size * row...]
    slice x2, local copies, waits for them, and re-layouts: 3.57 us -> 0.5 us  [on_device(): dw_kernel[offset]]
    dot_general x1, matrix products: 7.59 us -> 5.04 us  [expand_in(): jnp.dot(flat_rows, collect(w_in, 'fsdp', 0), preferred_element_type=jnp.f...]
  transfers between devices with their start and end apart: 2 -> 8, of which waited for: 2 -> 6; matrix products, arithmetic and copies ran while one was open for 23% -> 19% of each run, Pallas kernels for 0% -> 0%
where the time goes in v1:
time: 159 us; the launch traced here: 157 us
  waiting for transfers between devices  97.7 us (61%)
  other arithmetic  20.5 us (13%)
  between operations  13.7 us (9%)
  matrix products  9.97 us (6%)
  starting transfers between devices  9.81 us (6%)
  local copies, waits for them, and re-layouts  5.35 us (3%)
    ppermute x4, waiting for transfers between devices, collect(): from_left = lax.ppermute(from_left, axis, right)  94.1 us
    reduce_sum x2, other arithmetic, layer_norm(): center = values - jnp.mean(values, axis=-1, keepdims=True)  15.5 us
    ppermute x3, starting transfers between devices, collect(): from_right = lax.ppermute(from_right, axis, downward)  8.38 us
    dot_general x1, matrix products, expand_in(): jnp.dot(flat_rows, collect(w_in, 'fsdp', 0), preferred_element_type=jnp.f...  5.04 us
    dot_general x1, matrix products, contract_out(): jnp.dot(flat_rows, lax.all_gather(w_out, 'fsdp', axis=0, tiled=True), pre...  4.93 us
    ppermute x3, waiting for transfers between devices, collect(): from_right = lax.ppermute(from_right, axis, downward)  3.52 us
  transfers between devices with their start and end apart: 8, of which 6 were waited for; matrix products, arithmetic and copies ran while one was open for 19% of the time, Pallas kernels for 0%

profile of v1, /device:TPU:0, one launch (start us, length us, event | category | flops | bytes accessed | tf_op | source)
XLA Modules:
  0.0 157.1 jit_solution(100113233877723067)
XLA Ops:
  6.5 0.5 collective-permute-start
  7.0 2.9 %collective-permute-start.1 = (bf16[192,3072]{1,0:T(8,128)(2,1)}, bf16[192,3072]{1,0:T(8,128)(2,1)S(1)}, u32[]{:S(2)}, u32[]{:S(2)}) collective-permute-start(bf16[192,3072]{1,0:T(8,128)(2,1)} %param.10), channel_id=1, source_target_pairs={{0,7},{1,0},{2,1},{3,2},{4,3},{5,4},{6,5},{7,6},{8,15},{9,8},{10,9... | collective-permute-start | bytes 3538952 | tf_op jit(solution)/shard_map/ppermute | solution.py:19
  10.0 1.7 %convert_reduce_fusion = f32[2,256]{1,0:T(2,128)S(1)} fusion(bf16[2,256,1536]{2,1,0:T(8,128)(2,1)} %param.7), kind=kLoop, calls=%fused_computation.1 | loop fusion | flops 1572352 | bytes 1574912 | tf_op jit(solution)/shard_map/reduce_sum | solution.py:27
  11.7 28.7 %collective-permute-done = bf16[192,3072]{1,0:T(8,128)(2,1)} collective-permute-done((bf16[192,3072]{1,0:T(8,128)(2,1)}, bf16[192,3072]{1,0:T(8,128)(2,1)}, u32[]{:S(2)}, u32[]{:S(2)}) %collective-permute-start) | collective-permute-done | bytes 1179680 | tf_op jit(solution)/shard_map/ppermute | solution.py:16
  40.5 0.9 collective-permute-start.2
  41.4 0.5 fusion.2
  42.1 0.5 fusion.4
  42.6 1.7 %collective-permute-done.1 = bf16[192,3072]{1,0:T(8,128)(2,1)S(1)} collective-permute-done((bf16[192,3072]{1,0:T(8,128)(2,1)}, bf16[192,3072]{1,0:T(8,128)(2,1)S(1)}, u32[]{:S(2)}, u32[]{:S(2)}) %collective-permute-start.1) | collective-permute-done | bytes 1179680 | tf_op jit(solution)/shard_map/ppermute | solution.py:19
  44.4 2.8 %collective-permute-start.3 = (bf16[192,3072]{1,0:T(8,128)(2,1)S(1)}, bf16[192,3072]{1,0:T(8,128)(2,1)S(1)}, u32[]{:S(2)}, u32[]{:S(2)}) collective-permute-start(bf16[192,3072]{1,0:T(8,128)(2,1)S(1)} %collective-permute-done.1), channel_id=1, source_target_pairs={{0,7},{1,0},{2,1},{3,2},{4,3},{5,4},{6,5},{7,6},{8,15},{9,8},{10,9... | collective-permute-start | bytes 3538952 | tf_op jit(solution)/shard_map/ppermute | solution.py:19
  47.1 0.3 slice_reduce_fusion.30
  47.5 32.7 %collective-permute-done.2 = bf16[192,3072]{1,0:T(8,128)(2,1)} collective-permute-done((bf16[192,3072]{1,0:T(8,128)(2,1)}, bf16[192,3072]{1,0:T(8,128)(2,1)}, u32[]{:S(2)}, u32[]{:S(2)}) %collective-permute-start.2) | collective-permute-done | bytes 1179680 | tf_op jit(solution)/shard_map/ppermute | solution.py:16
  80.2 0.2 slice_reduce_fusion.29
  80.4 1.2 broadcast_in_dim.29
  81.8 1.4 constant_dynamic-update-slice_fusion.6
  83.2 2.7 %collective-permute-start.5 = (bf16[192,3072]{1,0:T(8,128)(2,1)S(1)}, bf16[192,3072]{1,0:T(8,128)(2,1)S(1)}, u32[]{:S(2)}, u32[]{:S(2)}) collective-permute-start(bf16[192,3072]{1,0:T(8,128)(2,1)S(1)} %collective-permute-done.3), channel_id=1, source_target_pairs={{0,7},{1,0},{2,1},{3,2},{4,3},{5,4},{6,5},{7,6},{8,15},{9,8},{10,9... | collective-permute-start | bytes 3538952 | tf_op jit(solution)/shard_map/ppermute | solution.py:19
  85.9 0.1 constant_dynamic-update-slice_fusion.5
  86.1 19.8 %collective-permute-done.4 = bf16[192,3072]{1,0:T(8,128)(2,1)S(1)} collective-permute-done((bf16[192,3072]{1,0:T(8,128)(2,1)}, bf16[192,3072]{1,0:T(8,128)(2,1)S(1)}, u32[]{:S(2)}, u32[]{:S(2)}) %collective-permute-start.4) | collective-permute-done | bytes 1179680 | tf_op jit(solution)/shard_map/ppermute | solution.py:16
  105.9 1.4 constant_dynamic-update-slice_fusion.4
  107.3 0.1 constant_dynamic-update-slice_fusion.3
  107.4 0.1 constant_dynamic-update-slice_fusion.2
  107.5 1.8 %collective-permute-done.5 = bf16[192,3072]{1,0:T(8,128)(2,1)S(1)} collective-permute-done((bf16[192,3072]{1,0:T(8,128)(2,1)S(1)}, bf16[192,3072]{1,0:T(8,128)(2,1)S(1)}, u32[]{:S(2)}, u32[]{:S(2)}) %collective-permute-start.5) | collective-permute-done | bytes 1179680 | tf_op jit(solution)/shard_map/ppermute | solution.py:19
  109.3 0.1 constant_dynamic-update-slice_fusion.1
  109.5 12.9 %collective-permute-done.6 = bf16[192,3072]{1,0:T(8,128)(2,1)S(1)} collective-permute-done((bf16[192,3072]{1,0:T(8,128)(2,1)S(1)}, bf16[192,3072]{1,0:T(8,128)(2,1)S(1)}, u32[]{:S(2)}, u32[]{:S(2)}) %collective-permute-start.6) | collective-permute-done | bytes 1179680 | tf_op jit(solution)/shard_map/ppermute | solution.py:16
  122.4 0.1 constant_dynamic-update-slice_fusion
  122.5 5.0 %fusion.11 = f32[512,3072]{1,0:T(8,128)S(1)} fusion(bf16[512,1536]{1,0:T(8,128)(2,1)S(1)} %bitcast.9, bf16[1536,3072]{1,0:T(8,128)(2,1)S(1)} %constant_dynamic-update-slice_fusion), kind=kOutput, calls=%fused_computation.72 | convolution fusion | flops 4831838208 | bytes 17301504 | tf_op jit(solution)/shard_map/dot_general | solution.py:34
  127.6 0.8 fusion.9
  128.4 0.2 broadcast_select_fusion.1
  128.6 13.8 %fusion.10 = (f32[2,256]{1,0:T(2,128)S(1)}, f32[2,256,1536]{2,1,0:T(8,128)S(1)}) fusion(f32[1536]{0:T(1024)S(1)} %get-tuple-element.34, f32[1536]{0:T(1024)S(1)} %get-tuple-element.35, f32[1536]{0:T(1024)S(1)} %get-tuple-element.6, f32[1536]{0:T(1024)S(1)} %get-tuple-element.7, f32[1536]{0:T(1024)S(1)} %get-tuple-element.8, f32[1536]{0:T(1024)S(1)} %get-tuple-element.9, ...), kind=kLoop, calls=%fused_computation.71 | loop fusion | flops 73137664 | bytes 4911104 | tf_op jit(solution)/shard_map/reduce_sum | solution.py:27
  142.4 0.4 multiply_reduce_fusion
  142.8 1.1 multiply_convert_fusion
  144.0 4.9 %convolution_convert_fusion = bf16[512,1536]{1,0:T(8,128)(2,1)S(1)} fusion(bf16[512,1536]{1,0:T(8,128)(2,1)S(1)} %bitcast.11, bf16[1536,1536]{1,0:T(8,128)(2,1)} %all-gather.2.cloned.1.call-done), kind=kOutput, calls=%fused_computation.16 | convolution fusion | flops 2416705536 | bytes 7864320 | tf_op jit(solution)/shard_map/dot_general | solution.py:41
  148.9 1.3 broadcast_select_fusion
  (24 shorter events, 0.4 us)
Async XLA Ops:
  6.5 34.9 %copy-start = (bf16[2,256,1536]{2,1,0:T(8,128)(2,1)S(1)}, bf16[2,256,1536]{2,1,0:T(8,128)(2,1)}, u32[]{:S(2)}) copy-start(bf16[2,256,1536]{2,1,0:T(8,128)(2,1)} %param.7) | copy-start | bytes 4718596
  6.5 35.6 %copy-start.3 = (f32[1536]{0:T(1024)S(1)}, f32[1536]{0:T(1024)}, u32[]{:S(2)}) copy-start(f32[1536]{0:T(1024)} %param.9) | copy-start | bytes 18436
  6.5 137.4 %all-gather.2.cloned.1.call-start = ((), (), s32[]{:S(2)}) async-start(), calls=%async_computation | async-start | bytes 5308416 | tf_op jit(solution)/shard_map/all_gather | solution.py:43
  6.5 33.9 %collective-permute-start = (bf16[192,3072]{1,0:T(8,128)(2,1)}, bf16[192,3072]{1,0:T(8,128)(2,1)}, u32[]{:S(2)}, u32[]{:S(2)}) collective-permute-start(bf16[192,3072]{1,0:T(8,128)(2,1)} %param.10), channel_id=1, source_target_pairs={{0,1},{1,2},{2,3},{3,4},{4,5},{5,6},{6,7},{7,0},{8,9},{9,10},{10,1... | collective-permute-start | bytes 3538952 | tf_op jit(solution)/shard_map/ppermute | solution.py:16
  7.0 37.3 %collective-permute-start.1 = (bf16[192,3072]{1,0:T(8,128)(2,1)}, bf16[192,3072]{1,0:T(8,128)(2,1)S(1)}, u32[]{:S(2)}, u32[]{:S(2)}) collective-permute-start(bf16[192,3072]{1,0:T(8,128)(2,1)} %param.10), channel_id=1, source_target_pairs={{0,7},{1,0},{2,1},{3,2},{4,3},{5,4},{6,5},{7,6},{8,15},{9,8},{10,9... | collective-permute-start | bytes 3538952 | tf_op jit(solution)/shard_map/ppermute | solution.py:19
  10.0 37.1 %copy-start.2 = (f32[31,1536]{1,0:T(8,128)S(1)}, f32[31,1536]{1,0:T(8,128)}, u32[]{:S(2)}) copy-start(f32[31,1536]{1,0:T(8,128)} %param.11) | copy-start | bytes 571396
  10.0 37.4 %copy-start.5 = (s32[2]{0:T(128)S(1)}, s32[2]{0:T(128)}, u32[]{:S(2)}) copy-start(s32[2]{0:T(128)} %param.8) | copy-start | bytes 28
  40.5 39.8 %collective-permute-start.2 = (bf16[192,3072]{1,0:T(8,128)(2,1)}, bf16[192,3072]{1,0:T(8,128)(2,1)}, u32[]{:S(2)}, u32[]{:S(2)}) collective-permute-start(bf16[192,3072]{1,0:T(8,128)(2,1)} %collective-permute-done), channel_id=1, source_target_pairs={{0,1},{1,2},{2,3},{3,4},{4,5},{5,6},{6,7},{7,0},{8,9},{9,10},{10,1... | collective-permute-start | bytes 3538952 | tf_op jit(solution)/shard_map/ppermute | solution.py:16
  44.4 38.9 %collective-permute-start.3 = (bf16[192,3072]{1,0:T(8,128)(2,1)S(1)}, bf16[192,3072]{1,0:T(8,128)(2,1)S(1)}, u32[]{:S(2)}, u32[]{:S(2)}) collective-permute-start(bf16[192,3072]{1,0:T(8,128)(2,1)S(1)} %collective-permute-done.1), channel_id=1, source_target_pairs={{0,7},{1,0},{2,1},{3,2},{4,3},{5,4},{6,5},{7,6},{8,15},{9,8},{10,9... | collective-permute-start | bytes 3538952 | tf_op jit(solution)/shard_map/ppermute | solution.py:19
  80.2 25.6 %collective-permute-start.4 = (bf16[192,3072]{1,0:T(8,128)(2,1)}, bf16[192,3072]{1,0:T(8,128)(2,1)S(1)}, u32[]{:S(2)}, u32[]{:S(2)}) collective-permute-start(bf16[192,3072]{1,0:T(8,128)(2,1)} %collective-permute-done.2), channel_id=1, source_target_pairs={{0,1},{1,2},{2,3},{3,4},{4,5},{5,6},{6,7},{7,0},{8,9},{9,10},{10,1... | collective-permute-start | bytes 3538952 | tf_op jit(solution)/shard_map/ppermute | solution.py:16
  80.4 1.3 copy-start.1
  83.2 26.1 %collective-permute-start.5 = (bf16[192,3072]{1,0:T(8,128)(2,1)S(1)}, bf16[192,3072]{1,0:T(8,128)(2,1)S(1)}, u32[]{:S(2)}, u32[]{:S(2)}) collective-permute-start(bf16[192,3072]{1,0:T(8,128)(2,1)S(1)} %collective-permute-done.3), channel_id=1, source_target_pairs={{0,7},{1,0},{2,1},{3,2},{4,3},{5,4},{6,5},{7,6},{8,15},{9,8},{10,9... | collective-permute-start | bytes 3538952 | tf_op jit(solution)/shard_map/ppermute | solution.py:19
  105.9 16.5 %collective-permute-start.6 = (bf16[192,3072]{1,0:T(8,128)(2,1)S(1)}, bf16[192,3072]{1,0:T(8,128)(2,1)S(1)}, u32[]{:S(2)}, u32[]{:S(2)}) collective-permute-start(bf16[192,3072]{1,0:T(8,128)(2,1)S(1)} %collective-permute-done.4), channel_id=1, source_target_pairs={{0,1},{1,2},{2,3},{3,4},{4,5},{5,6},{6,7},{7,0},{8,9},{9,10},{10,1... | collective-permute-start | bytes 3538952 | tf_op jit(solution)/shard_map/ppermute | solution.py:16
  128.6 14.3 %copy-start.4 = (f32[1536]{0:T(1024)S(1)}, f32[1536]{0:T(1024)}, u32[]{:S(2)}) copy-start(f32[1536]{0:T(1024)} %param.12) | copy-start | bytes 18436
Sparse Core Ops, SparseCore 0:
  10.1 56.1 all-gather.1
